TPU v7x, 256 devices: a whole 4x4x8 slice. The times are simulated.
256 devices in a mesh: row: 8 (over y, z_lo), col: 32 (over z_hi, x, core).
Axes of the slice: x: 4, y: 4, z: 8 (z_hi: 4, z_lo: 2; z = z_hi * 2 + z_lo), core: 2. Of those that a mesh axis runs over, the one named last changes fastest.
Arguments:
- grad_output: bfloat16 [1024, 8192], P('col', 'row'), may hold values from -6 to 6
- inputs: bfloat16 [1024, 28672], P('row', 'col'), may hold values from -0.1875 to 0.1875
- weight: bfloat16 [28672, 8192], P('col', 'row'), may hold values from -0.125 to 0.125
- block_mask: int32 [224, 64], P('col'), may hold values from 0 to 1, as said below
Outputs:
- grad_input: bfloat16 [1024, 28672], P('row', 'col')
- grad_weight: bfloat16 [28672, 8192], P('col', 'row')
Inputs may be any that keep to these rules, and one draw needn't show every extreme that they name: `block_mask`: 1 where the 128 x 128 block of weight is kept, 0 where it is zero; the share of kept blocks differs widely from block row to block row.
All inputs are finite; a program needn't handle non-finite values.
Results may differ from a plain program's by a relative error of at most 0.001.
Values may be sent and summed in bfloat16 or wider, within the bound.
A program may use at most 64 MiB of HBM per device.

v0:
```python
import jax
import jax.numpy as jnp
from jax import lax
from jax.sharding import PartitionSpec as P

BLOCK = 128


def joined_along(parts, dim):
    parts = jnp.moveaxis(parts, 0, dim)
    shape = parts.shape
    return parts.reshape(*shape[:dim], shape[dim] * shape[dim + 1], *shape[dim + 2 :])


def sent_to_all(x, axis):
    size = lax.axis_size(axis)
    return lax.all_to_all(jnp.broadcast_to(x[None], (size, *x.shape)), axis, 0, 0, tiled=True)


def gather_directly(x, axis, dim):
    return joined_along(sent_to_all(x, axis), dim)


def split_up(x, dim, size):
    shape = x.shape
    parts = x.reshape(*shape[:dim], size, shape[dim] // size, *shape[dim + 1 :])
    return jnp.moveaxis(parts, dim, 0)


def summed_on_arrival(x, axis, dim):
    size = lax.axis_size(axis)
    parts = lax.all_to_all(split_up(x, dim, size), axis, 0, 0, tiled=True)
    return jnp.sum(parts, axis=0)


def masked_tile(weight_tile, mask_tile):
    rows = weight_tile.shape[0]
    cols = weight_tile.shape[1]
    shaped = weight_tile.reshape(rows // BLOCK, BLOCK, cols // BLOCK, BLOCK)
    factor = mask_tile.astype(jnp.bfloat16)[:, None, :, None]
    return (shaped * factor).reshape(rows, cols)


def per_device(grad_output, inputs, weight, block_mask):
    grads_all = lax.all_gather(grad_output, "col", axis=0, tiled=True)
    inputs_all = gather_directly(inputs, "row", 0)
    tile_cols = weight.shape[1] // BLOCK
    mask_tile = lax.dynamic_slice_in_dim(
        block_mask, lax.axis_index("row") * tile_cols, tile_cols, 1
    )
    kept_tile = masked_tile(weight, mask_tile)
    partial_value = lax.dot_general(
        grads_all, kept_tile, (((1,), (1,)), ((), ())), preferred_element_type=jnp.float32
    )
    grad_input = summed_on_arrival(partial_value, "row", 0).astype(jnp.bfloat16)
    product = lax.dot_general(
        inputs_all, grads_all, (((0,), (0,)), ((), ())), preferred_element_type=jnp.float32
    )
    rows = product.shape[0]
    cols = product.shape[1]
    factor = mask_tile.astype(jnp.float32)[:, None, :, None]
    grad_weight = (
        (product.reshape(rows // BLOCK, BLOCK, cols // BLOCK, BLOCK) * factor)
        .reshape(rows, cols)
        .astype(jnp.bfloat16)
    )
    return (grad_input, grad_weight)


def solution(mesh):
    return jax.shard_map(
        per_device,
        mesh=mesh,
        in_specs=(P("col", "row"), P("row", "col"), P("col", "row"), P("col", None)),
        out_specs=(P("row", "col"), P("col", "row")),
        check_vma=False,
    )
```

profile of v0, /device:TPU:1, one launch (start us, length us, event | category | flops | bytes accessed | tf_op | source)
XLA Modules:
  0.0 135.1 jit_solution(849341611892757135)
XLA Ops:
  7.2 0.0 all-gather.2.cloned.1.call-start
  7.2 0.7 all-gather.2.cloned.1.call-update
  7.9 1.1 copy.19
  9.0 1.5 %broadcast_in_dim.2 = bf16[8,128,896]{1,2,0:T(8,128)(2,1)} broadcast(bf16[128,896]{0,1:T(8,128)(2,1)S(1)} %copy.19), dimensions={1,2} | broadcast | bytes 2064384 | tf_op jit(solution)/shard_map/broadcast_in_dim | solution.py:17
  10.5 0.0 copy-start.1
  10.5 6.5 %all-to-all-start.1 = ((bf16[8,128,896]{1,2,0:T(8,128)(2,1)}), bf16[8,128,896]{1,2,0:T(8,128)(2,1)S(1)}, u32[]{:S(2)}, u32[]{:S(2)}) async-start(bf16[8,128,896]{1,2,0:T(8,128)(2,1)} %broadcast_in_dim.2), calls=%async_computation.1 | async-start | bytes 3670016 | tf_op jit(solution)/shard_map/all_to_all | solution.py:17
  17.0 0.0 copy-done.1
  17.0 0.1 dynamic-slice_convert_fusion
  17.1 52.6 %all-gather.2.cloned.1.call-done = bf16[1024,1024]{1,0:T(8,128)(2,1)} async-done(((bf16[32,1024]{1,0:T(8,128)(2,1)}), bf16[1024,1024]{1,0:T(8,128)(2,1)}) %all-gather.2.cloned.1.call-update) | async-done | bytes 2097168 | tf_op jit(solution)/shard_map/all_gather | solution.py:45
  69.7 0.0 copy-start.2
  69.7 0.3 mul.23
  70.0 1.2 copy-done.2
  71.2 3.7 %convolution_bitcast_fusion = f32[112,8,8,128]{3,2,1,0:T(8,128)S(1)} fusion(bf16[1024,1024]{1,0:T(8,128)(2,1)} %all-gather.2.cloned.1.call-done, bf16[896,1024]{1,0:T(8,128)(2,1)S(1)} %copy-done.2, bf16[112,8,8,128]{3,2,1,0:T(8,128)(2,1)S(1)} %bitcast.38), kind=kOutput, calls=%fused_computation.2 | convolution fusion | flops 1879965696 | bytes 9437184 | tf_op jit(solution)/shard_map/dot_general | solution.py:52
  74.9 2.1 %copy.36 = f32[112,8,8,128]{3,2,0,1:T(8,128)} copy(f32[112,8,8,128]{3,2,1,0:T(8,128)S(1)} %convolution_bitcast_fusion) | data formatting | bytes 7340032 | tf_op jit(solution)/shard_map/reshape | solution.py:26
  77.0 0.0 all-to-all-done.1
  77.0 4.5 %all-to-all-start = ((f32[8,128,896]{1,2,0:T(8,128)}), f32[8,128,896]{1,2,0:T(8,128)}, u32[]{:S(2)}, u32[]{:S(2)}) async-start(f32[8,128,896]{1,2,0:T(8,128)} %bitcast.31), calls=%async_computation | async-start | bytes 7340032 | tf_op jit(solution)/shard_map/all_to_all | solution.py:32
  81.5 2.6 %copy.20 = bf16[8,128,896]{2,1,0:T(8,128)(2,1)} copy(bf16[8,128,896]{1,2,0:T(8,128)(2,1)S(1)} %all-to-all-done.1) | data formatting | bytes 3670016 | tf_op jit(solution)/shard_map/all_to_all | solution.py:17
  84.1 0.0 copy-start
  84.1 4.0 %copy.21 = bf16[896,1024]{1,0:T(8,128)(2,1)} copy(bf16[896,1024]{0,1:T(8,128)(2,1)} %bitcast.32) | data formatting | bytes 3670016 | tf_op jit(solution)/shard_map/dot_general | solution.py:56
  88.1 0.0 copy-done
  88.1 2.6 %copy.22 = bf16[1024,1024]{1,0:T(8,128)(2,1)} copy(bf16[1024,1024]{0,1:T(8,128)(2,1)S(1)} %bitcast.34) | data formatting | bytes 4194304 | tf_op jit(solution)/shard_map/dot_general | solution.py:56
  90.7 4.2 %multiply_convert_fusion = bf16[7,128,8,128]{3,1,2,0:T(8,128)(2,1)S(1)} fusion(bf16[7,128,1024,1]{2,1,3,0:T(8,128)(2,1)} %bitcast.37, bf16[8,128,1024,1]{2,1,0,3:T(8,128)(2,1)} %bitcast.35, f32[7,8]{1,0:T(8,128)S(1)} %get-tuple-element.6), kind=kOutput, calls=%fused_computation.1 | convolution fusion | flops 1880883200 | bytes 5767392 | tf_op jit(solution)/shard_map/dot_general | solution.py:56
  95.0 1.2 copy.23
  96.2 1.8 %copy.37 = bf16[112,8,8,128]{3,1,2,0:T(8,128)(2,1)} copy(bf16[112,8,8,128]{3,2,1,0:T(8,128)(2,1)S(1)} %bitcast.33) | data formatting | bytes 3670016
  97.9 27.2 %all-to-all-done = f32[8,128,896]{1,2,0:T(8,128)} async-done(((f32[8,128,896]{1,2,0:T(8,128)}), f32[8,128,896]{1,2,0:T(8,128)}, u32[]{:S(2)}, u32[]{:S(2)}) %all-to-all-start) | async-done | bytes 3670048 | tf_op jit(solution)/shard_map/all_to_all | solution.py:32
  125.2 2.2 %reduce_sum.9 = bf16[128,896]{0,1:T(8,128)(2,1)S(1)} reduce(f32[8,128,896]{1,2,0:T(8,128)} %all-to-all-done, f32[]{:T(128)} %constant.13.clone.1), dimensions={0}, to_apply=%region_0.0 | reduce | flops 802816 | bytes 3899396 | tf_op jit(solution)/shard_map/reduce_sum | solution.py:33
  127.4 0.8 copy.24
Async XLA Ops:
  7.2 62.5 %all-gather.2.cloned.1.call-start = ((), (), s32[]{:S(2)}) async-start(), calls=%async_computation.2 | async-start | bytes 2162688 | tf_op jit(solution)/shard_map/all_gather | solution.py:45
  10.5 6.5 %copy-start.1 = (s32[7,64]{1,0:T(8,128)S(1)}, s32[7,64]{1,0:T(8,128)}, u32[]{:S(2)}) copy-start(s32[7,64]{1,0:T(8,128)} %param.7) | copy-start | bytes 5380
  10.5 66.5 %all-to-all-start.1 = ((bf16[8,128,896]{1,2,0:T(8,128)(2,1)}), bf16[8,128,896]{1,2,0:T(8,128)(2,1)S(1)}, u32[]{:S(2)}, u32[]{:S(2)}) async-start(bf16[8,128,896]{1,2,0:T(8,128)(2,1)} %broadcast_in_dim.2), calls=%async_computation.1 | async-start | bytes 3670016 | tf_op jit(solution)/shard_map/all_to_all | solution.py:17
  69.7 1.5 %copy-start.2 = (bf16[896,1024]{1,0:T(8,128)(2,1)S(1)}, bf16[896,1024]{1,0:T(8,128)(2,1)}, u32[]{:S(2)}) copy-start(bf16[896,1024]{1,0:T(8,128)(2,1)} %param.6) | copy-start | bytes 5505028
  77.0 48.2 %all-to-all-start = ((f32[8,128,896]{1,2,0:T(8,128)}), f32[8,128,896]{1,2,0:T(8,128)}, u32[]{:S(2)}, u32[]{:S(2)}) async-start(f32[8,128,896]{1,2,0:T(8,128)} %bitcast.31), calls=%async_computation | async-start | bytes 7340032 | tf_op jit(solution)/shard_map/all_to_all | solution.py:32
  84.1 4.0 %copy-start = (bf16[1024,1024]{1,0:T(8,128)(2,1)S(1)}, bf16[1024,1024]{1,0:T(8,128)(2,1)}, u32[]{:S(2)}) copy-start(bf16[1024,1024]{1,0:T(8,128)(2,1)} %all-gather.2.cloned.1.call-done) | copy-start | bytes 6291460
Sparse Core Ops, SparseCore 0:
  10.5 59.1 all-gather.1
where the time goes:
time: 135 us
  waiting for transfers between devices  80.5 us (60%)
  local copies, waits for them, and re-layouts  19.1 us (14%)
  between operations  14.1 us (10%)
  starting transfers between devices  11 us (8%)
  matrix products  7.99 us (6%)
  other arithmetic  2.3 us (2%)
    all_gather x1, waiting for transfers between devices, per_device(): grads_all = lax.all_gather(grad_output, 'col', axis=0, tiled=True)  52.6 us
    all_to_all x1, waiting for transfers between devices, summed_on_arrival(): parts = lax.all_to_all(split_up(x, dim, size), axis, 0, 0, tiled=True)  27.2 us
    dot_general x2, local copies, waits for them, and re-layouts, per_device(): lax.dot_general(inputs_all, grads_all, (((0,), (0,)), ((), ())), preferre...  6.57 us
    all_to_all x1, starting transfers between devices, sent_to_all(): lax.all_to_all(jnp.broadcast_to(x[None], (size, *x.shape)), axis, 0, 0, t...  6.49 us
    unnamed x9, local copies, waits for them, and re-layouts  4.9 us
    all_to_all x1, starting transfers between devices, summed_on_arrival(): parts = lax.all_to_all(split_up(x, dim, size), axis, 0, 0, tiled=True)  4.5 us
    dot_general x1, matrix products, per_device(): lax.dot_general(inputs_all, grads_all, (((0,), (0,)), ((), ())), preferre...  4.25 us
    dot_general x1, matrix products, per_device(): lax.dot_general(grads_all, kept_tile, (((1,), (1,)), ((), ())), preferred...  3.75 us
  transfers between devices with their start and end apart: 3, of which 2 were waited for; matrix products, arithmetic and copies ran while one was open for 19% of the time, Pallas kernels for 0%

commit v1 on v0

v1 whole, which is shorter than its diff:
```python
import functools

import jax
import jax.numpy as jnp
from jax import lax
from jax.experimental import pallas as pl
from jax.experimental.pallas import tpu as pltpu
from jax.sharding import PartitionSpec as P

MESH = pl.DeviceIdType.MESH
BLOCK = 128
TOKENS = 1024
MINE = 32
ROWS = 128
ZFIRST = 64
PIECE = 32
TOP = 32767.0
RELAYED = (0, 1, -1)


def wrap(v, n):
    return lax.rem(v + n, n)


def kernel(
    g_hbm, in_hbm, w_hbm, mask_hbm, gi_out, gw_out,
    mask, gi_ref, gw_ref, gall, inall, flipped, kept, part,
    code_out, code_in, scale_out, scale_in,
    ssem, rsem, lsem,
):
    row, col = lax.axis_index("row"), lax.axis_index("col")
    y, zl = row // 2, lax.rem(row, 2)
    zh, x, k = col // 8, lax.rem(col // 2, 4), lax.rem(col, 2)
    hid, wid = w_hbm.shape

    def dev(dy=0, flip=False, dzh=0, dx=0, core=False):
        z = 1 - zl if flip else zl
        c = 1 - k if core else k
        return (wrap(y + dy, 4) * 2 + z, (wrap(zh + dzh, 4) * 4 + wrap(x + dx, 4)) * 2 + c)

    peers = [
        dev(dy=1), dev(dy=-1), dev(flip=True), dev(dzh=1), dev(dzh=-1),
        dev(dx=1), dev(dx=-1), dev(core=True),
    ]
    peers.append(dev(dx=2))

    load_g = pltpu.make_async_copy(
        g_hbm, gall.at[pl.ds(pl.multiple_of(col * MINE, MINE), MINE)], lsem.at[0]
    )
    load_in = pltpu.make_async_copy(
        in_hbm, inall.at[pl.ds(pl.multiple_of(row * ROWS, ROWS), ROWS)], lsem.at[1]
    )
    load_w = pltpu.make_async_copy(w_hbm, kept, lsem.at[2])
    load_mask = pltpu.make_async_copy(mask_hbm, mask, lsem.at[3])
    for load in (load_g, load_in, load_mask, load_w):
        load.start()

    barrier = pltpu.get_barrier_semaphore()
    for peer in peers:
        pl.semaphore_signal(barrier, inc=1, device_id=peer, device_id_type=MESH)
    pl.semaphore_wait(barrier, len(peers))
    load_g.wait()
    load_in.wait()

    kinds = {"g": gall, "in": inall, "code": code_out, "scale": scale_out}
    order = list(kinds)
    leading = dict.fromkeys(kinds, 0)
    names = {}

    def remote(kind, name, src, dst, device):
        i = names.setdefault(name, len(names))
        return pltpu.make_async_remote_copy(
            src_ref=src, dst_ref=dst, send_sem=ssem.at[order.index(kind)], recv_sem=rsem.at[i],
            device_id=device, device_id_type=MESH,
        )

    def send(kind, name, src, dst, device):
        leading[kind] += src.shape[0]
        remote(kind, name, src, dst, device).start()

    def arrived(name, ref):
        remote("g", name, ref, ref, dev(core=True)).wait_recv()

    def g(dz, dx, half=None):
        at = ((wrap(zh + dz, 4) * 4 + wrap(x + dx, 4)) * 2 + k) * MINE
        if half is None:
            return gall.at[pl.ds(pl.multiple_of(at, MINE), MINE)]
        n = MINE // 2
        return gall.at[pl.ds(pl.multiple_of(at + half * n, n), n)]

    def send_g(name, ref, device):
        send("g", name, ref, ref, device)

    def across(d, e):
        send_g("c", g(d, e), dev(core=True))

    def spread_x(d):
        send_g(("xp", d), g(d, 0), dev(dx=1))
        send_g(("xm", d), g(d, 0), dev(dx=-1))
        if d not in RELAYED:
            send_g(("x2", d), g(d, 0), dev(dx=2))
        across(d, 0)

    def relay_x(d):
        arrived(("xp", d), g(d, -1))
        if d in RELAYED:
            send_g(("x2", d), g(d, -1, 0), dev(dx=1))
        across(d, -1)
        arrived(("xm", d), g(d, 1))
        if d in RELAYED:
            send_g(("x2", d), g(d, 1, 1), dev(dx=-1))
        across(d, 1)

    def finish_x(d):
        arrived(("x2", d), g(d, 2))
        across(d, 2)

    def rows_in(dy, flip, lo, n):
        z = 1 - zl if flip else zl
        at = (wrap(y + dy, 4) * 2 + z) * ROWS + lo
        return inall.at[pl.ds(pl.multiple_of(at, 16), n)]

    def send_in(name, dy, flip, lo, n, device):
        ref = rows_in(dy, flip, lo, n)
        send("in", name, ref, ref, device)

    def spread_y(tag, flip, lo, n):
        send_in("iyp" + tag, 0, flip, lo, n, dev(dy=1))
        send_in("iym" + tag, 0, flip, lo, n, dev(dy=-1))

    def relay_y(tag, flip, lo, n):
        h = n // 2
        arrived("iyp" + tag, rows_in(-1, flip, lo, n))
        send_in("iy2" + tag, -1, flip, lo, h, dev(dy=1))
        arrived("iym" + tag, rows_in(1, flip, lo, n))
        send_in("iy2" + tag, 1, flip, lo + h, h, dev(dy=-1))

    zn, yn = ZFIRST, ROWS - ZFIRST

    send_g("zp", g(0, 0), dev(dzh=1))
    send_g("zm", g(0, 0), dev(dzh=-1))
    spread_x(0)
    spread_y("1", False, zn, yn)
    spread_y("0", False, 0, zn)
    send_in("iz", 0, False, 0, zn, dev(flip=True))

    load_mask.wait()
    load_w.wait()

    def mask_row(i, _):
        rows = pl.ds(pl.multiple_of(i * BLOCK, BLOCK), BLOCK)
        for j in range(wid // BLOCK):
            cols = pl.ds(j * BLOCK, BLOCK)
            m = mask[i, row * (wid // BLOCK) + j].astype(jnp.float32)
            kept[rows, cols] = (kept[rows, cols].astype(jnp.float32) * m).astype(jnp.bfloat16)
        return 0

    lax.fori_loop(0, hid // BLOCK, mask_row, 0)

    relay_x(0)
    arrived("zp", g(-1, 0))
    send_g("z2", g(-1, 0, 0), dev(dzh=1))
    spread_x(-1)
    arrived("zm", g(1, 0))
    send_g("z2", g(1, 0, 1), dev(dzh=-1))
    spread_x(1)
    relay_y("1", False, zn, yn)
    finish_x(0)
    relay_y("0", False, 0, zn)
    arrived("iz", rows_in(0, True, 0, zn))
    spread_y("2", True, 0, zn)
    relay_x(-1)
    arrived("z2", g(2, 0))
    spread_x(2)
    send_in("jz", 0, False, zn, yn, dev(flip=True))
    send_in("jz", -1, False, zn, yn, dev(flip=True))
    send_in("jz", 1, False, zn, yn, dev(flip=True))
    relay_x(1)
    arrived("iy21", rows_in(2, False, zn, yn))
    send_in("jz", 2, False, zn, yn, dev(flip=True))
    finish_x(-1)
    finish_x(1)
    relay_x(2)
    relay_y("2", True, 0, zn)
    finish_x(2)
    arrived("c", gall.at[pl.ds(0, TOKENS // 2)])

    def multiply(i, dy):
        tokens = gall[pl.ds(pl.multiple_of(wrap(y + dy, 4) * 256, 256), 256), :]
        for lo in range(0, hid, 256):
            n = min(256, hid - lo)
            part[i, :, pl.ds(lo, n)] = lax.dot_general(
                tokens, kept[pl.ds(lo, n), :], (((1,), (1,)), ((), ())),
                preferred_element_type=jnp.float32,
            )

    def piece(i, q, w, late=0):
        z = zl if q else 1 - zl
        at = z * ROWS + late * 2 * PIECE + w * PIECE
        return part[i, pl.ds(pl.multiple_of(at, PIECE), PIECE), :]

    slots = {}
    used = [0, 0]

    def post(name, sem, values, device):
        c, m, n = slots[name] = (used[0], used[1], len(values))
        used[0] += n
        used[1] += 1
        top = functools.reduce(
            jnp.maximum, [jnp.max(jnp.abs(v), axis=0, keepdims=True) for v in values]
        )
        top = jnp.maximum(top, 1e-30)
        scale_out[m] = top * (1.0 / TOP)
        for j, v in enumerate(values):
            code_out[c + j] = jnp.round(v * (TOP / top)).astype(jnp.int32).astype(jnp.int16)
        cs, ms = pl.ds(c, n), pl.ds(m, 1)
        send("scale", (sem, "s"), scale_out.at[ms], scale_in.at[ms], device)
        send("code", (sem, "q"), code_out.at[cs], code_in.at[cs], device)

    def wait_for(sem, messages, n):
        arrived((sem, "s"), scale_in.at[pl.ds(0, messages)])
        arrived((sem, "q"), code_in.at[pl.ds(0, messages * n)])

    def decode(name, j=0):
        c, m, _ = slots[name]
        return code_in[c + j].astype(jnp.int32).astype(jnp.float32) * scale_in[m]

    ways = ((0, 1, 1), (1, 3, -1))

    def first(qs):
        for w, _, s in ways:
            post(("m1", qs, w), ("m1", qs), [piece(2, q, w) for q in qs], dev(dy=s))

    def second(qs, way):
        w, i, s = way
        post(("m2", qs, w), ("m2", qs), [piece(i, q, 1 - w) for q in qs], dev(dy=s))

    def third(qs):
        wait_for(("m1", qs), 2, len(qs))
        for w, i, s in ways:
            values = [piece(i, q, w) + decode(("m1", qs, w), j) for j, q in enumerate(qs)]
            post(("m3", qs, w), ("m3", qs), values, dev(dy=s))

    def settle(qs):
        wait_for(("m2", qs), 2, len(qs))
        wait_for(("m3", qs), 2, len(qs))

    def here(qs, q, w):
        j = qs.index(q)
        return piece(0, q, w) + decode(("m2", qs, 1 - w), j) + decode(("m3", qs, w), j)

    def cross(i, w):
        post(("x", i, w), ("x", i, w), [piece(i, 0, w, 1)], dev(flip=True))

    def crossed(i, w):
        wait_for(("x", i, w), 1, 1)
        return piece(i, 1, w, 1) + decode(("x", i, w))

    def late_first():
        for w, _, s in ways:
            post(("n1", w), "n1", [crossed(2, w)], dev(dy=s))

    def late_second():
        for w, i, s in ways:
            post(("n2", w), "n2", [crossed(i, 1 - w)], dev(dy=s))

    def late_third():
        wait_for("n1", 2, 1)
        for w, i, s in ways:
            post(("n3", w), "n3", [crossed(i, w) + decode(("n1", w))], dev(dy=s))

    def store(w, late, total):
        gi_ref[pl.ds(late * 2 * PIECE + w * PIECE, PIECE), :] = total.astype(jnp.bfloat16)

    both, theirs, ours = (0, 1), (0,), (1,)

    multiply(2, 2)
    cross(2, 0)
    cross(2, 1)
    first(both)
    multiply(1, 1)
    second(both, ways[0])
    cross(1, 1)
    multiply(3, -1)
    cross(3, 0)
    second(both, ways[1])
    cross(1, 0)
    cross(3, 1)
    multiply(0, 0)
    cross(0, 0)
    cross(0, 1)
    third(both)
    late_first()
    late_second()

    arrived("iy20", rows_in(2, False, 0, zn))
    arrived("iy22", rows_in(2, True, 0, zn))
    arrived("jz", inall.at[pl.ds(0, 4 * yn)])

    def flip(i, _):
        rows = pl.ds(pl.multiple_of(i * BLOCK, BLOCK), BLOCK)
        for j in range(hid // BLOCK):
            cols = pl.ds(j * BLOCK, BLOCK)
            flipped[cols, rows] = inall[rows, cols].T
        return 0

    lax.fori_loop(0, TOKENS // BLOCK, flip, 0)

    def weight_grad(n, _):
        right = gall[:, pl.ds(pl.multiple_of(n * 256, 256), 256)]
        for i in range(hid // BLOCK):
            rows = pl.ds(i * BLOCK, BLOCK)
            product = jnp.dot(flipped[rows, :], right, preferred_element_type=jnp.float32)
            for j in range(2):
                m = mask[i, row * (wid // BLOCK) + n * 2 + j].astype(jnp.float32)
                gw_ref[rows, pl.ds(pl.multiple_of(n * 256 + j * BLOCK, BLOCK), BLOCK)] = (
                    product[:, j * BLOCK : (j + 1) * BLOCK] * m
                ).astype(jnp.bfloat16)
        return 0

    lax.fori_loop(0, wid // 256, weight_grad, 0)
    store_gw = pltpu.make_async_copy(gw_ref, gw_out, lsem.at[2])
    store_gw.start()

    settle(both)
    post("mz", "mz", [here(both, 0, w) for w in (0, 1)], dev(flip=True))
    late_third()
    wait_for("n2", 2, 1)
    wait_for("n3", 2, 1)
    for w in (0, 1):
        store(w, 1, crossed(0, w) + decode(("n2", 1 - w)) + decode(("n3", w)))
    wait_for("mz", 1, 2)
    for w in (0, 1):
        store(w, 0, here(both, 1, w) + decode("mz", w))
    store_gi = pltpu.make_async_copy(gi_ref, gi_out, lsem.at[0])
    store_gi.start()

    for kind, ref in kinds.items():
        sent = ref.at[pl.ds(0, leading[kind])]
        remote(kind, "c", sent, sent, dev(core=True)).wait_send()
    store_gw.wait()
    store_gi.wait()


def put(gi, gw, gi_out, gw_out, sem):
    n = gw.shape[0] // 7
    copies = [pltpu.make_async_copy(gi, gi_out, sem.at[7])]
    for i in range(7):
        rows = pl.ds(i * n, n)
        copies.append(pltpu.make_async_copy(gw.at[rows], gw_out.at[rows], sem.at[i]))
    for c in copies:
        c.start()
    for c in copies:
        c.wait()


def per_device(grad_output, inputs, weight, block_mask):
    hid, wid = weight.shape
    anywhere = pl.BlockSpec(memory_space=pl.ANY)
    near = pl.BlockSpec(memory_space=pltpu.VMEM)
    codes = [pltpu.VMEM((28, PIECE, hid), jnp.int16)] * 2
    scales = [pltpu.VMEM((24, 1, hid), jnp.float32)] * 2
    results = pl.pallas_call(
        kernel,
        out_shape=(pltpu.VMEM((ROWS, hid), jnp.bfloat16), pltpu.VMEM((hid, wid), jnp.bfloat16)),
        in_specs=[anywhere] * 4,
        out_specs=(anywhere, anywhere),
        scratch_shapes=[
            pltpu.SMEM(block_mask.shape, jnp.int32),
            pltpu.VMEM((ROWS, hid), jnp.bfloat16),
            pltpu.VMEM((hid, wid), jnp.bfloat16),
            pltpu.VMEM((TOKENS, wid), jnp.bfloat16),
            pltpu.VMEM((TOKENS, hid), jnp.bfloat16),
            pltpu.VMEM((hid, TOKENS), jnp.bfloat16),
            pltpu.VMEM((hid, wid), jnp.bfloat16),
            pltpu.VMEM((4, 256, hid), jnp.float32),
            *codes,
            *scales,
            pltpu.SemaphoreType.DMA((4,)),
            pltpu.SemaphoreType.DMA((60,)),
            pltpu.SemaphoreType.DMA((4,)),
        ],
        compiler_params=pltpu.CompilerParams(
            collective_id=0, has_side_effects=True, vmem_limit_bytes=56 << 20
        ),
        name="down_projection_backward",
    )(grad_output, inputs, weight, block_mask)
    return pl.pallas_call(
        put,
        out_shape=(
            jax.ShapeDtypeStruct((ROWS, hid), jnp.bfloat16),
            jax.ShapeDtypeStruct((hid, wid), jnp.bfloat16),
        ),
        in_specs=[near, near],
        out_specs=(anywhere, anywhere),
        scratch_shapes=[pltpu.SemaphoreType.DMA((8,))],
        name="put",
    )(*(pltpu.with_memory_space_constraint(r, pltpu.VMEM) for r in results))


def solution(mesh):
    return jax.shard_map(
        per_device,
        mesh=mesh,
        in_specs=(P("col", "row"), P("row", "col"), P("col", "row"), P("col", None)),
        out_specs=(P("row", "col"), P("col", "row")),
        check_vma=False,
    )
```

time: 135 us -> 45.6 us (0.34)
  the two profiles are of different devices: /device:TPU:1 before, /device:TPU:32 now
where the time goes in v1:
time: 45.6 us; the launch traced here: 45.5 us
  Pallas kernels  44.9 us (98%)
  between operations  0.64 us (1%)
    pallas_call x1, Pallas kernels, per_device(): pl.pallas_call(kernel, out_shape=(pltpu.VMEM((ROWS, hid), jnp.bfloat16),...  43.5 us
    pallas_call x1, Pallas kernels, per_device(): pl.pallas_call(put, out_shape=(jax.ShapeDtypeStruct((ROWS, hid), jnp.bflo...  1.37 us

profile of v1, /device:TPU:32, one launch (start us, length us, event | category | flops | bytes accessed | tf_op | source)
XLA Modules:
  0.0 45.5 jit_solution(5312980146740263133)
XLA Ops:
  0.6 43.5 %down_projection_backward.1 = (bf16[128,896]{1,0:T(8,128)(2,1)S(1)}, bf16[896,1024]{1,0:T(8,128)(2,1)S(1)}) custom-call(bf16[32,1024]{1,0:T(8,128)(2,1)} %g_hbm.1, bf16[128,896]{1,0:T(8,128)(2,1)} %in_hbm.1, bf16[896,1024]{1,0:T(8,128)(2,1)} %w_hbm.1, s32[7,64]{1,0:T(8,128)} %mask_hbm.1), custom_call_target="tpu_custom_call" | custom-call | tf_op jit(solution)/shard_map/down_projection_backward/pallas_call | solution.py:363
  44.2 1.4 %put.1 = (bf16[128,896]{1,0:T(8,128)(2,1)}, bf16[896,1024]{1,0:T(8,128)(2,1)}) custom-call(bf16[128,896]{1,0:T(8,128)(2,1)S(1)} %get-tuple-element.4.gi, bf16[896,1024]{1,0:T(8,128)(2,1)S(1)} %get-tuple-element.5.gw), custom_call_target="tpu_custom_call" | custom-call | tf_op jit(solution)/shard_map/put/pallas_call | solution.py:388

commit v2 on v1

--- a/solution.py
+++ b/solution.py
@@ -15,7 +15,7 @@
 ZFIRST = 64
 PIECE = 32
 TOP = 32767.0
-RELAYED = (0, 1, -1)
+RELAYED = (1, -1)
 
 
 def wrap(v, n):
@@ -24,7 +24,7 @@
 
 def kernel(
     g_hbm, in_hbm, w_hbm, mask_hbm, gi_out, gw_out,
-    mask, gi_ref, gw_ref, gall, inall, flipped, kept, part,
+    mask, gi_ref, gw_ref, gall, inall, flipped, kept, part, grad,
     code_out, code_in, scale_out, scale_in,
     ssem, rsem, lsem,
 ):
@@ -94,22 +94,37 @@
     def across(d, e):
         send_g("c", g(d, e), dev(core=True))
 
-    def spread_x(d):
-        send_g(("xp", d), g(d, 0), dev(dx=1))
-        send_g(("xm", d), g(d, 0), dev(dx=-1))
+    def spread_z():
+        for name, dz, part in (("zp", 1, 0), ("zm", -1, 1), ("zp", 1, 1), ("zm", -1, 0)):
+            send_g((name, part), g(0, 0, part), dev(dzh=dz))
+
+    def spread_x(d, part=None):
+        send_g(("xp", d, part), g(d, 0, part), dev(dx=1))
+        send_g(("xm", d, part), g(d, 0, part), dev(dx=-1))
         if d not in RELAYED:
-            send_g(("x2", d), g(d, 0), dev(dx=2))
-        across(d, 0)
-
-    def relay_x(d):
-        arrived(("xp", d), g(d, -1))
-        if d in RELAYED:
-            send_g(("x2", d), g(d, -1, 0), dev(dx=1))
-        across(d, -1)
-        arrived(("xm", d), g(d, 1))
-        if d in RELAYED:
-            send_g(("x2", d), g(d, 1, 1), dev(dx=-1))
-        across(d, 1)
+            send_g(("x2", d), g(d, 0, part), dev(dx=2))
+        send_g("c", g(d, 0, part), dev(core=True))
+
+    def near_z():
+        for name, d, part, on in (("zp", -1, 0, 1), ("zm", 1, 1, -1), ("zp", -1, 1, 0), ("zm", 1, 0, 0)):
+            arrived((name, part), g(d, 0, part))
+            if on:
+                send_g("z2", g(d, 0, part), dev(dzh=on))
+            spread_x(d, part)
+
+    def near_x(d):
+        halves = abs(d) == 1
+        for name, e, part in (("xp", -1, 0), ("xm", 1, 1)):
+            if halves:
+                arrived((name, d, part), g(d, e, part))
+            else:
+                arrived((name, d, None), g(d, e))
+            if d in RELAYED:
+                send_g(("x2", d), g(d, e, part), dev(dx=-e))
+        for name, e, part in (("xp", -1, 1), ("xm", 1, 0)):
+            if halves:
+                arrived((name, d, part), g(d, e, part))
+            across(d, e)
 
     def finish_x(d):
         arrived(("x2", d), g(d, 2))
@@ -118,7 +133,7 @@
     def rows_in(dy, flip, lo, n):
         z = 1 - zl if flip else zl
         at = (wrap(y + dy, 4) * 2 + z) * ROWS + lo
-        return inall.at[pl.ds(pl.multiple_of(at, 16), n)]
+        return inall.at[pl.ds(pl.multiple_of(at, 8), n)]
 
     def send_in(name, dy, flip, lo, n, device):
         ref = rows_in(dy, flip, lo, n)
@@ -137,12 +152,11 @@
 
     zn, yn = ZFIRST, ROWS - ZFIRST
 
-    send_g("zp", g(0, 0), dev(dzh=1))
-    send_g("zm", g(0, 0), dev(dzh=-1))
+    spread_z()
     spread_x(0)
     spread_y("1", False, zn, yn)
     spread_y("0", False, 0, zn)
-    send_in("iz", 0, False, 0, zn, dev(flip=True))
+    send_in("iza", 0, False, 0, zn // 2, dev(flip=True))
 
     load_mask.wait()
     load_w.wait()
@@ -157,31 +171,30 @@
 
     lax.fori_loop(0, hid // BLOCK, mask_row, 0)
 
-    relay_x(0)
-    arrived("zp", g(-1, 0))
-    send_g("z2", g(-1, 0, 0), dev(dzh=1))
-    spread_x(-1)
-    arrived("zm", g(1, 0))
-    send_g("z2", g(1, 0, 1), dev(dzh=-1))
-    spread_x(1)
+    near_x(0)
+    near_z()
+    send_in("izb", 0, False, zn // 2, zn // 2, dev(flip=True))
     relay_y("1", False, zn, yn)
     finish_x(0)
     relay_y("0", False, 0, zn)
-    arrived("iz", rows_in(0, True, 0, zn))
-    spread_y("2", True, 0, zn)
-    relay_x(-1)
+    arrived("iza", rows_in(0, True, 0, zn // 2))
+    spread_y("2", True, 0, zn // 2)
+    near_x(-1)
     arrived("z2", g(2, 0))
     spread_x(2)
+    arrived("izb", rows_in(0, True, zn // 2, zn // 2))
+    spread_y("3", True, zn // 2, zn // 2)
     send_in("jz", 0, False, zn, yn, dev(flip=True))
     send_in("jz", -1, False, zn, yn, dev(flip=True))
     send_in("jz", 1, False, zn, yn, dev(flip=True))
-    relay_x(1)
+    near_x(1)
     arrived("iy21", rows_in(2, False, zn, yn))
     send_in("jz", 2, False, zn, yn, dev(flip=True))
     finish_x(-1)
     finish_x(1)
-    relay_x(2)
-    relay_y("2", True, 0, zn)
+    near_x(2)
+    relay_y("2", True, 0, zn // 2)
+    relay_y("3", True, zn // 2, zn // 2)
     finish_x(2)
     arrived("c", gall.at[pl.ds(0, TOKENS // 2)])
 
@@ -236,18 +249,12 @@
         post(("m2", qs, w), ("m2", qs), [piece(i, q, 1 - w) for q in qs], dev(dy=s))
 
     def third(qs):
-        wait_for(("m1", qs), 2, len(qs))
         for w, i, s in ways:
-            values = [piece(i, q, w) + decode(("m1", qs, w), j) for j, q in enumerate(qs)]
+            values = [piece(i, q, w) + decode(("m1", both, w), q) for q in qs]
             post(("m3", qs, w), ("m3", qs), values, dev(dy=s))
 
-    def settle(qs):
-        wait_for(("m2", qs), 2, len(qs))
-        wait_for(("m3", qs), 2, len(qs))
-
-    def here(qs, q, w):
-        j = qs.index(q)
-        return piece(0, q, w) + decode(("m2", qs, 1 - w), j) + decode(("m3", qs, w), j)
+    def here(q, w):
+        return piece(0, q, w) + decode(("m2", both, 1 - w), q) + decode(("m3", (q,), w))
 
     def cross(i, w):
         post(("x", i, w), ("x", i, w), [piece(i, 0, w, 1)], dev(flip=True))
@@ -271,6 +278,53 @@
 
     def store(w, late, total):
         gi_ref[pl.ds(late * 2 * PIECE + w * PIECE, PIECE), :] = total.astype(jnp.bfloat16)
+
+    def tokens(i, flip, lo, n):
+        z = 1 - zl if flip else zl
+        return pl.ds(pl.multiple_of((i * 2 + z) * ROWS + lo, 16), n)
+
+    early = [tokens(i, False, 0, ROWS) for i in range(4)] + [tokens(i, True, 0, zn) for i in range(4)]
+    late = [tokens(i, True, zn, yn) for i in range(4)]
+    n_early = 4 * (ROWS + zn)
+
+    def turn(groups, at):
+        def turn_cols(j, _):
+            cols = pl.ds(pl.multiple_of(j * BLOCK, BLOCK), BLOCK)
+            for i, group in enumerate(groups):
+                rows = jnp.concatenate([inall[t, cols] for t in group], axis=0)
+                flipped[cols, pl.ds(at + i * BLOCK, BLOCK)] = rows.T
+            return 0
+
+        lax.fori_loop(0, hid // BLOCK, turn_cols, 0)
+
+    def blocks(parts, n):
+        c = BLOCK // n
+        return [parts[i : i + c] for i in range(0, len(parts), c)]
+
+    def early_grad(n, _):
+        cols = pl.ds(pl.multiple_of(n * 256, 256), 256)
+        right = jnp.concatenate([gall[t, cols] for t in early], axis=0)
+        for i in range(0, hid, BLOCK):
+            rows = pl.ds(i, BLOCK)
+            grad[rows, cols] = jnp.dot(
+                flipped[rows, pl.ds(0, n_early)], right, preferred_element_type=jnp.float32
+            )
+        return 0
+
+    def late_grad(n, _):
+        cols = pl.ds(pl.multiple_of(n * 256, 256), 256)
+        right = jnp.concatenate([gall[t, cols] for t in late], axis=0)
+        for i in range(hid // BLOCK):
+            rows = pl.ds(i * BLOCK, BLOCK)
+            product = grad[rows, cols] + jnp.dot(
+                flipped[rows, pl.ds(n_early, 4 * yn)], right, preferred_element_type=jnp.float32
+            )
+            for j in range(2):
+                m = mask[i, row * (wid // BLOCK) + n * 2 + j].astype(jnp.float32)
+                gw_ref[rows, pl.ds(pl.multiple_of(n * 256 + j * BLOCK, BLOCK), BLOCK)] = (
+                    product[:, j * BLOCK : (j + 1) * BLOCK] * m
+                ).astype(jnp.bfloat16)
+        return 0
 
     both, theirs, ours = (0, 1), (0,), (1,)
 
@@ -289,49 +343,37 @@
     multiply(0, 0)
     cross(0, 0)
     cross(0, 1)
-    third(both)
+    arrived("iy20", rows_in(2, False, 0, zn))
+    arrived("iy22", rows_in(2, True, 0, zn // 2))
+    arrived("iy23", rows_in(2, True, zn // 2, zn // 2))
+    turn([[t] for t in early[:4]] + blocks(early[4:], zn), 0)
+    lax.fori_loop(0, 2, early_grad, 0)
+    wait_for(("m1", both), 2, 2)
+    third(theirs)
     late_first()
+    third(ours)
     late_second()
-
-    arrived("iy20", rows_in(2, False, 0, zn))
-    arrived("iy22", rows_in(2, True, 0, zn))
+    lax.fori_loop(2, wid // 256, early_grad, 0)
+
+    wait_for(("m2", both), 2, 2)
+    wait_for(("m3", theirs), 2, 1)
+    post("mz", "mz", [here(0, w) for w in (0, 1)], dev(flip=True))
+    late_third()
+
     arrived("jz", inall.at[pl.ds(0, 4 * yn)])
-
-    def flip(i, _):
-        rows = pl.ds(pl.multiple_of(i * BLOCK, BLOCK), BLOCK)
-        for j in range(hid // BLOCK):
-            cols = pl.ds(j * BLOCK, BLOCK)
-            flipped[cols, rows] = inall[rows, cols].T
-        return 0
-
-    lax.fori_loop(0, TOKENS // BLOCK, flip, 0)
-
-    def weight_grad(n, _):
-        right = gall[:, pl.ds(pl.multiple_of(n * 256, 256), 256)]
-        for i in range(hid // BLOCK):
-            rows = pl.ds(i * BLOCK, BLOCK)
-            product = jnp.dot(flipped[rows, :], right, preferred_element_type=jnp.float32)
-            for j in range(2):
-                m = mask[i, row * (wid // BLOCK) + n * 2 + j].astype(jnp.float32)
-                gw_ref[rows, pl.ds(pl.multiple_of(n * 256 + j * BLOCK, BLOCK), BLOCK)] = (
-                    product[:, j * BLOCK : (j + 1) * BLOCK] * m
-                ).astype(jnp.bfloat16)
-        return 0
-
-    lax.fori_loop(0, wid // 256, weight_grad, 0)
+    turn(blocks(late, yn), n_early)
+    lax.fori_loop(0, wid // 256, late_grad, 0)
     store_gw = pltpu.make_async_copy(gw_ref, gw_out, lsem.at[2])
     store_gw.start()
 
-    settle(both)
-    post("mz", "mz", [here(both, 0, w) for w in (0, 1)], dev(flip=True))
-    late_third()
     wait_for("n2", 2, 1)
     wait_for("n3", 2, 1)
     for w in (0, 1):
         store(w, 1, crossed(0, w) + decode(("n2", 1 - w)) + decode(("n3", w)))
+    wait_for(("m3", ours), 2, 1)
     wait_for("mz", 1, 2)
     for w in (0, 1):
-        store(w, 0, here(both, 1, w) + decode("mz", w))
+        store(w, 0, here(1, w) + decode("mz", w))
     store_gi = pltpu.make_async_copy(gi_ref, gi_out, lsem.at[0])
     store_gi.start()
 
@@ -359,7 +401,7 @@
     anywhere = pl.BlockSpec(memory_space=pl.ANY)
     near = pl.BlockSpec(memory_space=pltpu.VMEM)
     codes = [pltpu.VMEM((28, PIECE, hid), jnp.int16)] * 2
-    scales = [pltpu.VMEM((24, 1, hid), jnp.float32)] * 2
+    scales = [pltpu.VMEM((28, 1, hid), jnp.float32)] * 2
     results = pl.pallas_call(
         kernel,
         out_shape=(pltpu.VMEM((ROWS, hid), jnp.bfloat16), pltpu.VMEM((hid, wid), jnp.bfloat16)),
@@ -374,10 +416,11 @@
             pltpu.VMEM((hid, TOKENS), jnp.bfloat16),
             pltpu.VMEM((hid, wid), jnp.bfloat16),
             pltpu.VMEM((4, 256, hid), jnp.float32),
+            pltpu.VMEM((hid, wid), jnp.float32),
             *codes,
             *scales,
             pltpu.SemaphoreType.DMA((4,)),
-            pltpu.SemaphoreType.DMA((60,)),
+            pltpu.SemaphoreType.DMA((80,)),
             pltpu.SemaphoreType.DMA((4,)),
         ],
         compiler_params=pltpu.CompilerParams(

time: 45.6 us -> 43.9 us (0.963)
  the two profiles are of different devices: /device:TPU:32 before, /device:TPU:1 now
where the time goes in v2:
time: 43.9 us; the launch traced here: 43.8 us
  Pallas kernels  43.2 us (98%)
  between operations  0.64 us (1%)
    pallas_call x1, Pallas kernels, per_device(): pl.pallas_call(kernel, out_shape=(pltpu.VMEM((ROWS, hid), jnp.bfloat16),...  41.8 us
    pallas_call x1, Pallas kernels, per_device(): pl.pallas_call(put, out_shape=(jax.ShapeDtypeStruct((ROWS, hid), jnp.bflo...  1.37 us

profile of v2, /device:TPU:1, one launch (start us, length us, event | category | flops | bytes accessed | tf_op | source)
XLA Modules:
  0.0 43.8 jit_solution(15936117758276495716)
XLA Ops:
  0.6 41.8 %down_projection_backward.1 = (bf16[128,896]{1,0:T(8,128)(2,1)S(1)}, bf16[896,1024]{1,0:T(8,128)(2,1)S(1)}) custom-call(bf16[32,1024]{1,0:T(8,128)(2,1)} %g_hbm.1, bf16[128,896]{1,0:T(8,128)(2,1)} %in_hbm.1, bf16[896,1024]{1,0:T(8,128)(2,1)} %w_hbm.1, s32[7,64]{1,0:T(8,128)} %mask_hbm.1), custom_call_target="tpu_custom_call" | custom-call | tf_op jit(solution)/shard_map/down_projection_backward/pallas_call | solution.py:405
  42.4 1.4 %put.1 = (bf16[128,896]{1,0:T(8,128)(2,1)}, bf16[896,1024]{1,0:T(8,128)(2,1)}) custom-call(bf16[128,896]{1,0:T(8,128)(2,1)S(1)} %get-tuple-element.4.gi, bf16[896,1024]{1,0:T(8,128)(2,1)S(1)} %get-tuple-element.5.gw), custom_call_target="tpu_custom_call" | custom-call | tf_op jit(solution)/shard_map/put/pallas_call | solution.py:431

commit v3 on v2

--- a/solution.py
+++ b/solution.py
@@ -156,7 +156,6 @@
     spread_x(0)
     spread_y("1", False, zn, yn)
     spread_y("0", False, 0, zn)
-    send_in("iza", 0, False, 0, zn // 2, dev(flip=True))
 
     load_mask.wait()
     load_w.wait()
@@ -173,6 +172,7 @@
 
     near_x(0)
     near_z()
+    send_in("iza", 0, False, 0, zn // 2, dev(flip=True))
     send_in("izb", 0, False, zn // 2, zn // 2, dev(flip=True))
     relay_y("1", False, zn, yn)
     finish_x(0)
@@ -180,6 +180,7 @@
     arrived("iza", rows_in(0, True, 0, zn // 2))
     spread_y("2", True, 0, zn // 2)
     near_x(-1)
+    near_x(1)
     arrived("z2", g(2, 0))
     spread_x(2)
     arrived("izb", rows_in(0, True, zn // 2, zn // 2))
@@ -187,7 +188,6 @@
     send_in("jz", 0, False, zn, yn, dev(flip=True))
     send_in("jz", -1, False, zn, yn, dev(flip=True))
     send_in("jz", 1, False, zn, yn, dev(flip=True))
-    near_x(1)
     arrived("iy21", rows_in(2, False, zn, yn))
     send_in("jz", 2, False, zn, yn, dev(flip=True))
     finish_x(-1)
@@ -227,12 +227,11 @@
         for j, v in enumerate(values):
             code_out[c + j] = jnp.round(v * (TOP / top)).astype(jnp.int32).astype(jnp.int16)
         cs, ms = pl.ds(c, n), pl.ds(m, 1)
-        send("scale", (sem, "s"), scale_out.at[ms], scale_in.at[ms], device)
-        send("code", (sem, "q"), code_out.at[cs], code_in.at[cs], device)
+        send("scale", sem, scale_out.at[ms], scale_in.at[ms], device)
+        send("code", sem, code_out.at[cs], code_in.at[cs], device)
 
     def wait_for(sem, messages, n):
-        arrived((sem, "s"), scale_in.at[pl.ds(0, messages)])
-        arrived((sem, "q"), code_in.at[pl.ds(0, messages * n)])
+        arrived(sem, scale_in.at[pl.ds(0, messages * (n * PIECE // 2 + 1))])
 
     def decode(name, j=0):
         c, m, _ = slots[name]
@@ -283,8 +282,10 @@
         z = 1 - zl if flip else zl
         return pl.ds(pl.multiple_of((i * 2 + z) * ROWS + lo, 16), n)
 
-    early = [tokens(i, False, 0, ROWS) for i in range(4)] + [tokens(i, True, 0, zn) for i in range(4)]
-    late = [tokens(i, True, zn, yn) for i in range(4)]
+    step = 32
+    early = [tokens(i, False, lo, step) for i in range(4) for lo in range(0, ROWS, step)]
+    early += [tokens(i, True, lo, step) for i in range(4) for lo in range(0, zn, step)]
+    late = [tokens(i, True, lo, step) for i in range(4) for lo in range(zn, ROWS, step)]
     n_early = 4 * (ROWS + zn)
 
     def turn(groups, at):
@@ -297,8 +298,8 @@
 
         lax.fori_loop(0, hid // BLOCK, turn_cols, 0)
 
-    def blocks(parts, n):
-        c = BLOCK // n
+    def blocks(parts):
+        c = BLOCK // step
         return [parts[i : i + c] for i in range(0, len(parts), c)]
 
     def early_grad(n, _):
@@ -346,7 +347,7 @@
     arrived("iy20", rows_in(2, False, 0, zn))
     arrived("iy22", rows_in(2, True, 0, zn // 2))
     arrived("iy23", rows_in(2, True, zn // 2, zn // 2))
-    turn([[t] for t in early[:4]] + blocks(early[4:], zn), 0)
+    turn(blocks(early), 0)
     lax.fori_loop(0, 2, early_grad, 0)
     wait_for(("m1", both), 2, 2)
     third(theirs)
@@ -361,7 +362,7 @@
     late_third()
 
     arrived("jz", inall.at[pl.ds(0, 4 * yn)])
-    turn(blocks(late, yn), n_early)
+    turn(blocks(late), n_early)
     lax.fori_loop(0, wid // 256, late_grad, 0)
     store_gw = pltpu.make_async_copy(gw_ref, gw_out, lsem.at[2])
     store_gw.start()
@@ -385,11 +386,10 @@
 
 
 def put(gi, gw, gi_out, gw_out, sem):
-    n = gw.shape[0] // 7
-    copies = [pltpu.make_async_copy(gi, gi_out, sem.at[7])]
-    for i in range(7):
-        rows = pl.ds(i * n, n)
-        copies.append(pltpu.make_async_copy(gw.at[rows], gw_out.at[rows], sem.at[i]))
+    copies = [
+        pltpu.make_async_copy(gw, gw_out, sem.at[0]),
+        pltpu.make_async_copy(gi, gi_out, sem.at[1]),
+    ]
     for c in copies:
         c.start()
     for c in copies:
@@ -401,7 +401,7 @@
     anywhere = pl.BlockSpec(memory_space=pl.ANY)
     near = pl.BlockSpec(memory_space=pltpu.VMEM)
     codes = [pltpu.VMEM((28, PIECE, hid), jnp.int16)] * 2
-    scales = [pltpu.VMEM((28, 1, hid), jnp.float32)] * 2
+    scales = [pltpu.VMEM((n, 1, hid), jnp.float32) for n in (23, 66)]
     results = pl.pallas_call(
         kernel,
         out_shape=(pltpu.VMEM((ROWS, hid), jnp.bfloat16), pltpu.VMEM((hid, wid), jnp.bfloat16)),
@@ -420,7 +420,7 @@
             *codes,
             *scales,
             pltpu.SemaphoreType.DMA((4,)),
-            pltpu.SemaphoreType.DMA((80,)),
+            pltpu.SemaphoreType.DMA((53,)),
             pltpu.SemaphoreType.DMA((4,)),
         ],
         compiler_params=pltpu.CompilerParams(
@@ -436,7 +436,7 @@
         ),
         in_specs=[near, near],
         out_specs=(anywhere, anywhere),
-        scratch_shapes=[pltpu.SemaphoreType.DMA((8,))],
+        scratch_shapes=[pltpu.SemaphoreType.DMA((2,))],
         name="put",
     )(*(pltpu.with_memory_space_constraint(r, pltpu.VMEM) for r in results))
 

time: 43.9 us -> 43.7 us (level)
  no operation moved by 1% of the time
where the time goes in v3:
time: 43.7 us; the launch traced here: 43.6 us
  Pallas kernels  42.9 us (98%)
  between operations  0.64 us (1%)
    pallas_call x1, Pallas kernels, per_device(): pl.pallas_call(kernel, out_shape=(pltpu.VMEM((ROWS, hid), jnp.bfloat16),...  41.6 us
    pallas_call x1, Pallas kernels, per_device(): pl.pallas_call(put, out_shape=(jax.ShapeDtypeStruct((ROWS, hid), jnp.bflo...  1.31 us

profile of v3, /device:TPU:1, one launch (start us, length us, event | category | flops | bytes accessed | tf_op | source)
XLA Modules:
  0.0 43.6 jit_solution(10473659379819132568)
XLA Ops:
  0.6 41.6 %down_projection_backward.1 = (bf16[128,896]{1,0:T(8,128)(2,1)S(1)}, bf16[896,1024]{1,0:T(8,128)(2,1)S(1)}) custom-call(bf16[32,1024]{1,0:T(8,128)(2,1)} %g_hbm.1, bf16[128,896]{1,0:T(8,128)(2,1)} %in_hbm.1, bf16[896,1024]{1,0:T(8,128)(2,1)} %w_hbm.1, s32[7,64]{1,0:T(8,128)} %mask_hbm.1), custom_call_target="tpu_custom_call" | custom-call | tf_op jit(solution)/shard_map/down_projection_backward/pallas_call | solution.py:405
  42.3 1.3 %put.1 = (bf16[128,896]{1,0:T(8,128)(2,1)}, bf16[896,1024]{1,0:T(8,128)(2,1)}) custom-call(bf16[128,896]{1,0:T(8,128)(2,1)S(1)} %get-tuple-element.4.gi, bf16[896,1024]{1,0:T(8,128)(2,1)S(1)} %get-tuple-element.5.gw), custom_call_target="tpu_custom_call" | custom-call | tf_op jit(solution)/shard_map/put/pallas_call | solution.py:431
